TPU v7x, 256 devices: a whole 4x4x8 slice. The times are simulated.
256 devices in a mesh: text: 32 (over z_lo, y, core), video: 8 (over x, z_hi).
Axes of the slice: x: 4, y: 4, z: 8 (z_hi: 2, z_lo: 4; z = z_hi * 4 + z_lo), core: 2. Of those that a mesh axis runs over, the one named last changes fastest.
Arguments:
- queries: bfloat16 [4096, 4096], P('text'), may hold values from -53 to 53
- video_keys: bfloat16 [2048, 512], P('video'), may hold values from -6 to 6
- video_values: bfloat16 [2048, 512], P('video'), may hold values from -6 to 6
- grad_out: bfloat16 [4096, 4096], P('text'), may hold values from -6 to 6
- positions: int32 [4096], P('text'), may hold values from 1 to 2047, as said below
- span_bounds: int32 [32, 2], P('text'), may hold values from 0 to 2048, as said below
Outputs:
- attended: bfloat16 [4096, 4096], P('text', 'video')
- grad_query: bfloat16 [4096, 4096], P('text', 'video')
- grad_key: bfloat16 [2048, 512], P(('video', 'text'))
- grad_value: bfloat16 [2048, 512], P(('video', 'text'))
Inputs may be any that keep to these rules, and one draw needn't show every extreme that they name: `span_bounds`: column 0 is a multiple of 128 from 0 to 384; column 1 is a multiple of 128 from 1664 to 2048. `positions`: each position is at least its block's span start plus 1.
All inputs are finite; a program needn't handle non-finite values.
Results may differ from a plain program's by a relative error of at most 0.017.
Values sent between devices are 32-bit elements; how exact they have to be, the bound alone decides.
No kernel may reach another device: no remote copies, remote signals or barrier semaphores. Data moves between devices by JAX's collectives and lax.ppermute only.
A program may use at most 128 MiB of HBM per device.

v0:
```python
import jax
import jax.numpy as jnp
from jax import lax
from jax.sharding import PartitionSpec as P

H = 32
G = 4
HD = 128
TBLK = 128


masked_floor = -1e30


def widen(stats):
    return jnp.repeat(stats, HD, axis=1)


def local(queries, video_keys, video_values, grad_out, positions, span_bounds):
    row_count = queries.shape[0]
    video_count = video_keys.shape[0]
    per_group = H // G
    score_scale = HD ** (-0.5)
    video_rank = lax.axis_index("video")
    video_size = lax.axis_size("video")
    columns = video_rank * video_count + jnp.arange(video_count, dtype=jnp.int32)
    lower_rows = jnp.repeat(span_bounds[:, 0], TBLK, total_repeat_length=row_count)
    upper_rows = jnp.repeat(span_bounds[:, 1], TBLK, total_repeat_length=row_count)
    visible = (
        (columns[None, :] >= lower_rows[:, None])
        & (columns[None, :] < upper_rows[:, None])
        & (columns[None, :] <= positions[:, None])
    )[:, None, :]

    def group_parts(group):
        head_start = group * per_group * HD
        head_stop = (group + 1) * per_group * HD
        query_grp = queries[:, head_start:head_stop].reshape(row_count, per_group, HD)
        grad_grp = grad_out[:, head_start:head_stop].reshape(row_count, per_group, HD)
        key_grp = video_keys[:, group * HD : (group + 1) * HD]
        value_grp = video_values[:, group * HD : (group + 1) * HD]
        scores = (
            jnp.einsum("rhd,cd->rhc", query_grp, key_grp, preferred_element_type=jnp.float32)
            * score_scale
        )
        masked = jnp.where(visible, scores, masked_floor)
        return (query_grp, grad_grp, key_grp, value_grp, masked)

    peaks, totals, partial_value = ([], [], [])
    for group in range(G):
        query_grp, grad_grp, key_grp, value_grp, masked = group_parts(group)
        block_peak = jnp.max(masked, axis=2)
        weights = jnp.where(visible, jnp.exp(masked - block_peak[:, :, None]), 0.0)
        peaks.append(block_peak)
        totals.append(jnp.sum(weights, axis=2))
        partial_value.append(
            jnp.einsum(
                "rhc,cd->rhd",
                weights.astype(jnp.bfloat16),
                value_grp,
                preferred_element_type=jnp.float32,
            ).reshape(row_count, per_group * HD)
        )
    local_peak = jnp.concatenate(peaks, axis=1)
    local_total = jnp.concatenate(totals, axis=1)
    local_out = jnp.concatenate(partial_value, axis=1)
    width = H * HD // video_size
    row_top = lax.pmax(local_peak, "video")
    factor = jnp.exp(local_peak - row_top)
    numer, denom = lax.psum((local_out * widen(factor), local_total * factor), "video")
    attended_all = (numer / widen(denom)).astype(jnp.bfloat16)
    log_norm = row_top + jnp.log(denom)
    delta = jnp.sum(
        (grad_out.astype(jnp.float32) * attended_all.astype(jnp.float32)).reshape(row_count, H, HD),
        axis=2,
    )
    attended = lax.dynamic_slice_in_dim(attended_all, video_rank * width, width, 1)
    grads_query, grads_key, grads_value = ([], [], [])
    for group in range(G):
        query_grp, grad_grp, key_grp, value_grp, masked = group_parts(group)
        norm_grp = log_norm[:, group * per_group : (group + 1) * per_group]
        delta_grp = delta[:, group * per_group : (group + 1) * per_group]
        prob = jnp.where(visible, jnp.exp(masked - norm_grp[:, :, None]), 0.0)
        dprob = jnp.einsum("rhd,cd->rhc", grad_grp, value_grp, preferred_element_type=jnp.float32)
        dscore = (prob * (dprob - delta_grp[:, :, None])).astype(jnp.bfloat16)
        grads_query.append(
            jnp.einsum("rhc,cd->rhd", dscore, key_grp, preferred_element_type=jnp.float32).reshape(
                row_count, per_group * HD
            )
            * score_scale
        )
        grads_key.append(
            jnp.einsum("rhc,rhd->cd", dscore, query_grp, preferred_element_type=jnp.float32)
            * score_scale
        )
        grads_value.append(
            jnp.einsum(
                "rhc,rhd->cd",
                prob.astype(jnp.bfloat16),
                grad_grp,
                preferred_element_type=jnp.float32,
            )
        )
    query_terms = jnp.concatenate(grads_query, axis=1)
    key_terms = jnp.concatenate(grads_key, axis=1)
    value_terms = jnp.concatenate(grads_value, axis=1)
    grad_query = lax.psum_scatter(query_terms, "video", scatter_dimension=1, tiled=True).astype(
        jnp.bfloat16
    )
    key_sum, value_sum = (
        lax.psum_scatter(key_terms, "text", scatter_dimension=0, tiled=True),
        lax.psum_scatter(value_terms, "text", scatter_dimension=0, tiled=True),
    )
    return (attended, grad_query, key_sum.astype(jnp.bfloat16), value_sum.astype(jnp.bfloat16))


def solution(mesh):
    placed = (
        P("text", None),
        P("video", None),
        P("video", None),
        P("text", None),
        P("text"),
        P("text", None),
    )
    return jax.shard_map(
        local,
        mesh=mesh,
        in_specs=placed,
        out_specs=(
            P("text", "video"),
            P("text", "video"),
            P(("video", "text"), None),
            P(("video", "text"), None),
        ),
        check_vma=False,
    )
```

profile of v0, /device:TPU:8, one launch (start us, length us, event | category | flops | bytes accessed | tf_op | source)
XLA Modules:
  0.0 613.9 jit_solution(15111671909918039596)
XLA Ops:
  8.1 2.0 fusion.107
  11.0 1.3 compare_and_fusion.1
  14.2 1.4 fusion.113
  15.6 1.8 copy.160
  17.4 1.4 fusion.114
  18.9 2.2 fusion.33
  21.0 1.2 fusion.35
  22.2 1.2 fusion.37
  23.5 1.4 fusion.17
  24.9 1.2 fusion.39
  26.1 55.8 %pmax.7 = f32[128,32]{0,1:T(8,128)S(1)} all-reduce(f32[128,32]{0,1:T(8,128)S(1)} %pad_maximum_fusion.3), channel_id=1, replica_groups=mesh['text'=32,'video'=8] {'video'}, use_global_device_ids=true, to_apply=%region_4.6 | all-reduce | flops 4096 | bytes 32768 | tf_op jit(solution)/shard_map/pmax | solution.py:68
  82.0 2.0 copy.97
  84.0 2.0 copy.96
  86.1 2.0 copy.95
  88.1 2.0 copy.94
  91.7 3.1 bitcast_multiply_fusion
  94.8 2.2 fusion.106
  97.0 1.8 copy.165
  98.8 1.8 copy.164
  100.6 1.8 copy.163
  102.4 1.8 copy.162
  104.2 60.2 %psum.15 = f32[128,32]{0,1:T(8,128)S(1)} all-reduce(f32[128,32]{0,1:T(8,128)S(1)} %get-tuple-element.63), channel_id=1, replica_groups=mesh['text'=32,'video'=8] {'video'}, use_global_device_ids=true, to_apply=%region_10.12 | all-reduce | flops 4096 | bytes 32768 | tf_op jit(solution)/shard_map/psum | solution.py:70
  164.4 1.7 convolution_bitcast_fusion
  166.2 1.3 convolution_bitcast_fusion.1
  169.1 2.1 copy.152
  171.6 115.2 %all-reduce.2.cloned.1.call-done = f32[128,4096]{1,0:T(8,128)} async-done(((f32[128,4096]{1,0:T(8,128)}), f32[128,4096]{1,0:T(8,128)}) %all-reduce.2.cloned.1.call-update) | async-done | bytes 2097168 | tf_op jit(solution)/shard_map/psum | solution.py:70
  287.9 4.6 multiply_bitcast_fusion
  292.5 1.7 copy.168
  294.2 2.2 reduce_sum.49
  298.1 2.6 fusion.12
  300.7 0.9 copy.113
  301.6 2.2 fusion.11
  303.8 1.0 copy.108
  304.8 2.3 fusion.10
  307.1 1.3 fusion.16
  308.5 1.3 fusion.15
  309.8 1.3 fusion.14
  311.1 1.4 fusion.9
  312.7 1.0 copy.150
  313.7 1.1 convolution_multiply_fusion.4
  315.0 1.2 convolution_multiply_fusion.5
  316.4 1.0 copy.122
  318.5 1.5 pad_maximum_fusion
  320.0 22.5 %reduce-scatter.12.cloned.1.call-done = f32[8,512]{1,0:T(8,128)} async-done(((f32[256,512]{1,0:T(8,128)}), f32[8,512]{1,0:T(8,128)}) %reduce-scatter.12.cloned.1.call-update) | async-done | bytes 16400
  344.1 1.6 constant_dynamic-slice_fusion
  345.6 158.0 %reduce-scatter.10.cloned.1.call-done = f32[8,512]{1,0:T(8,128)} async-done(((f32[256,512]{1,0:T(8,128)}), f32[8,512]{1,0:T(8,128)}) %reduce-scatter.10.cloned.1.call-update) | async-done | bytes 16400
  505.2 99.5 %reduce-scatter.8.cloned.1.call-done = f32[128,512]{1,0:T(8,128)} async-done(((f32[128,4096]{1,0:T(8,128)}), f32[128,512]{1,0:T(8,128)}) %reduce-scatter.8.cloned.1.call-update) | async-done | bytes 262160 | tf_op jit(solution)/shard_map/reduce_scatter | solution.py:107
  604.7 1.6 convert_element_type.65
  (87 shorter events, 14.1 us)
Async XLA Ops:
  8.0 2.3 copy-start.21
  8.0 4.4 copy-start.22
  8.0 4.4 copy-start.14
  8.0 278.7 %all-reduce.2.cloned.1.call-start = ((), (), s32[]{:S(2)}) async-start(), calls=%async_computation.3 | async-start | bytes 4194304 | tf_op jit(solution)/shard_map/psum | solution.py:70
  11.0 3.2 copy-start.2
  17.4 3.6 copy-start.19
  18.8 4.6 copy-start
  90.1 1.0 copy-start.6
  90.1 1.2 copy-start.7
  90.1 1.4 copy-start.8
  90.1 1.5 copy-start.9
  94.8 247.7 %reduce-scatter.12.cloned.1.call-start = ((), (), s32[]{:S(2)}) async-start(), calls=%async_computation.6 | async-start | bytes 540672
  164.4 3.1 copy-start.18
  164.4 3.5 copy-start.16
  171.2 332.4 %reduce-scatter.10.cloned.1.call-start = ((), (), s32[]{:S(2)}) async-start(), calls=%async_computation.5 | async-start | bytes 540672
  286.7 1.2 copy-start.1
  300.7 6.4 %copy-start.20 = (f32[128,8]{1,0:T(8,128)S(1)}, f32[128,8]{1,0:T(8,128)}, u32[]{:S(2)}) copy-start(f32[128,8]{1,0:T(8,128)} %get-tuple-element.73) | copy-start | bytes 12292
  303.8 3.3 copy-start.5
  303.8 4.6 copy-start.4
  303.8 5.9 copy-start.3
  304.8 6.3 %copy-start.17 = (bf16[128,1024]{0,1:T(8,128)(2,1)S(1)}, bf16[128,1024]{0,1:T(8,128)(2,1)}, u32[]{:S(2)}) copy-start(bf16[128,1024]{0,1:T(8,128)(2,1)} %copy.162) | copy-start | bytes 786436
  311.1 2.7 copy-start.12
  312.7 2.3 copy-start.10
  314.9 2.5 copy-start.11
  314.9 2.5 copy-start.15
  314.9 289.8 %reduce-scatter.8.cloned.1.call-start = ((), (), s32[]{:S(2)}) async-start(), calls=%async_computation.4 | async-start | bytes 2359296 | tf_op jit(solution)/shard_map/reduce_scatter | solution.py:107
  317.4 1.0 copy-start.13
Sparse Core Ops, SparseCore 0:
  94.9 191.7 all-reduce.1
Sparse Core Ops, SparseCore 1:
  171.3 171.1 reduce-scatter.11
  344.9 158.7 reduce-scatter.9
  507.6 97.1 reduce-scatter.7
where the time goes:
time: 615 us; the launch traced here: 614 us
  waiting for transfers between devices  395 us (64%)
  blocking collectives  116 us (19%)
  local copies, waits for them, and re-layouts  40.7 us (7%)
  matrix products  28.9 us (5%)
  other arithmetic  16.7 us (3%)
  between operations  16.1 us (3%)
    unnamed x6, waiting for transfers between devices  181 us
    psum x1, waiting for transfers between devices, local(): lax.psum((local_out * widen(factor), local_total * factor), 'video')  115 us
    reduce_scatter x1, waiting for transfers between devices, local(): lax.psum_scatter(query_terms, 'video', scatter_dimension=1, tiled=True)  99.5 us
    psum x1, blocking collectives, local(): lax.psum((local_out * widen(factor), local_total * factor), 'video')  60.2 us
    pmax x1, blocking collectives, local(): row_top = lax.pmax(local_peak, 'video')  55.8 us
    unnamed x61, local copies, waits for them, and re-layouts  19.7 us
  transfers between devices with their start and end apart: 4, of which 4 were waited for; matrix products, arithmetic and copies ran while one was open for 9% of the time, Pallas kernels for 0%

commit v1 on v0

v1 whole, which is shorter than its diff:
```python
import jax
import jax.numpy as jnp
from jax import lax
from jax.experimental import pallas as pl
from jax.experimental.pallas import tpu as pltpu
from jax.sharding import Mesh, PartitionSpec as P

H = 32
G = 4
HD = 128
ROWS = 128
HL = 4
VID = 256
TOK = 2048
HALF = TOK // 2
CH = 256
NCH = HALF // CH
R = HL * ROWS
SCALE = HD ** (-0.5)
LOG2E = 1.4426950408889634
FLOOR = -1e30

PLANE = ("zl", "y", "x", "zh")


def kernel(info, q_ref, g_ref, own_ref, oth_ref, pos_ref, att_ref, dq_ref, down_ref, doth_ref, s_ref, e_ref, k_ref, v_ref):
    f32, bf16 = jnp.float32, jnp.bfloat16
    core, low, top = info[0], info[1], info[2]
    last = jnp.minimum(pos_ref[...], top - 1)
    q = jnp.concatenate([q_ref[:, h * HD : (h + 1) * HD] for h in range(HL)], axis=0)
    halves = ((own_ref, down_ref), (oth_ref, doth_ref))

    peak = jnp.full((1, R), FLOOR, f32)
    for n in range(2 * NCH):
        half, j = divmod(n, NCH)
        src = halves[half][0]
        tiles = slice(j * (CH // 8), (j + 1) * (CH // 8))
        key = src[tiles, 0].reshape(CH, HD).astype(bf16)
        k_ref[n * CH : (n + 1) * CH, :] = key
        v_ref[n * CH : (n + 1) * CH, :] = src[tiles, 1].reshape(CH, HD).astype(bf16)
        cc = core if half == 0 else 1 - core
        i = lax.broadcasted_iota(jnp.int32, (CH, ROWS), 0) + j * CH
        col = (((i >> 3) & 7) << 8) + ((i >> 6) << 4) + (i & 7) + cc * 8
        vis = (col >= low) & (col <= last)
        s = lax.dot_general(key, q, (((1,), (1,)), ((), ())), preferred_element_type=f32)
        tops = []
        for h in range(HL):
            sh = jnp.where(vis, s[:, h * ROWS : (h + 1) * ROWS], FLOOR)
            s_ref[n * CH : (n + 1) * CH, h * ROWS : (h + 1) * ROWS] = sh
            tops.append(jnp.max(sh, axis=0, keepdims=True))
        peak = jnp.maximum(peak, jnp.concatenate(tops, axis=1))

    total = jnp.zeros((1, R), f32)
    out_t = jnp.zeros((HD, R), f32)
    for n in range(2 * NCH):
        rows = slice(n * CH, (n + 1) * CH)
        e = jnp.exp2((s_ref[rows, :] - peak) * (SCALE * LOG2E))
        total = total + jnp.sum(e, axis=0, keepdims=True)
        s_ref[rows, :] = e
        low_e = e.astype(bf16)
        e_ref[rows, :] = low_e
        out_t = out_t + jnp.dot(v_ref[rows, :].T, low_e, preferred_element_type=f32)

    inv = 1.0 / total
    att_t = (out_t * inv).astype(bf16)
    g_t = jnp.concatenate([g_ref[:, h * HD : (h + 1) * HD].T for h in range(HL)], axis=1).astype(f32)
    delta = jnp.sum(g_t * att_t.astype(f32), axis=0, keepdims=True) * inv
    for h in range(HL):
        att_ref[:, h * HD : (h + 1) * HD] = att_t[:, h * ROWS : (h + 1) * ROWS].T
    g_t = (g_t * inv).astype(bf16)

    dq_t = jnp.zeros((HD, R), f32)
    for n in range(2 * NCH):
        half, j = divmod(n, NCH)
        dst = halves[half][1]
        tiles = slice(j * (CH // 8), (j + 1) * (CH // 8))
        rows = slice(n * CH, (n + 1) * CH)
        dp = jnp.dot(v_ref[rows, :], g_t, preferred_element_type=f32)
        ds = (s_ref[rows, :] * (dp - delta)).astype(bf16)
        dk = jnp.dot(ds, q, preferred_element_type=f32) * SCALE
        dv = lax.dot_general(e_ref[rows, :], g_t, (((1,), (1,)), ((), ())), preferred_element_type=f32)
        dst[tiles, 0] = dk.reshape(CH // 8, 8, HD)
        dst[tiles, 1] = dv.reshape(CH // 8, 8, HD)
        dq_t = dq_t + jnp.dot(k_ref[rows, :].T, ds, preferred_element_type=f32)
    for h in range(HL):
        dq_ref[:, h * HD : (h + 1) * HD] = (dq_t[:, h * ROWS : (h + 1) * ROWS] * SCALE).T.astype(bf16)


def attend(info, queries, grad_out, own, oth, pos):
    shape = (HALF // 8, 2, 8, HD)
    whole = pl.BlockSpec(shape, lambda i, info: (0, 0, 0, 0))
    heads = pl.BlockSpec((ROWS, HL * HD), lambda i, info: (0, info[3]))
    flat = pl.BlockSpec((ROWS, HL * HD), lambda i, info: (0, 0))
    return pl.pallas_call(
        kernel,
        out_shape=(
            jax.ShapeDtypeStruct((ROWS, HL * HD), jnp.bfloat16),
            jax.ShapeDtypeStruct((ROWS, HL * HD), jnp.bfloat16),
            jax.ShapeDtypeStruct(shape, jnp.float32),
            jax.ShapeDtypeStruct(shape, jnp.float32),
        ),
        grid_spec=pltpu.PrefetchScalarGridSpec(
            num_scalar_prefetch=1,
            grid=(1,),
            in_specs=[heads, heads, whole, whole, pl.BlockSpec((1, ROWS), lambda i, info: (0, 0))],
            out_specs=(flat, flat, whole, whole),
            scratch_shapes=[
                pltpu.VMEM((TOK, R), jnp.float32),
                pltpu.VMEM((TOK, R), jnp.bfloat16),
                pltpu.VMEM((TOK, HD), jnp.bfloat16),
                pltpu.VMEM((TOK, HD), jnp.bfloat16),
            ],
        ),
        name="attend",
    )(info, queries, grad_out, own, oth, pos)


def swap(x):
    return lax.ppermute(x, "c", [(0, 1), (1, 0)])


def local(queries, video_keys, video_values, grad_out, positions, span_bounds):
    zl, y, c = lax.axis_index("zl"), lax.axis_index("y"), lax.axis_index("c")
    x, zh = lax.axis_index("x"), lax.axis_index("zh")
    t = (zl * 4 + y) * 2 + c
    share = jnp.stack(
        [lax.dynamic_slice_in_dim(a, t * 8, 8, 0) for a in (video_keys, video_values)]
    ).astype(jnp.float32)
    share = share.reshape(2, 8, G, HD).transpose(2, 0, 1, 3)
    send = jnp.broadcast_to(share[None, :, None], (16, G, 2, 2, 8, HD)).reshape(128, 2, 8, HD)
    own = lax.all_to_all(send, PLANE, 0, 0, tiled=True)
    oth = swap(own)
    info = jnp.stack([c, span_bounds[0, 0], span_bounds[0, 1], x * 2 + zh]).astype(jnp.int32)
    att, dq, down, doth = attend(info, queries, grad_out, own, oth, positions.reshape(1, ROWS))
    part = down + swap(doth)
    got = lax.all_to_all(part, PLANE, 0, 0, tiled=True)
    got = got.reshape(16, G, 2, 2, 8, HD)
    got = jnp.sum(got, axis=(0, 2))
    got = got.transpose(1, 2, 0, 3).reshape(2, 8, G * HD).astype(jnp.bfloat16)
    return att, dq, got[0], got[1]


def solution(mesh):
    fine = Mesh(mesh.devices.reshape(4, 4, 2, 4, 2), ("zl", "y", "c", "x", "zh"))
    text, video = ("zl", "y", "c"), ("x", "zh")
    return jax.shard_map(
        local,
        mesh=fine,
        in_specs=(P(text, None), P(video, None), P(video, None), P(text, None), P(text), P(text, None)),
        out_specs=(P(text, video), P(text, video), P(video + text, None), P(video + text, None)),
        check_vma=False,
    )
```

time: 615 us -> 102 us (0.17)
  waiting for transfers between devices: 395 us -> 2.5 us
  local copies, waits for them, and re-layouts: 40.7 us -> 3.71 us
  blocking collectives: 116 us -> 82.7 us
  matrix products: 28.9 us -> 0 us
  between operations: 16.1 us -> 0.66 us
  other arithmetic: 16.7 us -> 3.34 us
  Pallas kernels: 0 us -> 8.2 us
    unnamed x6 -> x0, waiting for transfers between devices: 181 us -> none
    psum x1 -> x0, waiting for transfers between devices: 115 us -> none  [local(): lax.psum((local_out * widen(factor), local_total * factor), 'video')]
    reduce_scatter x1 -> x0, waiting for transfers between devices: 99.5 us -> none  [local(): lax.psum_scatter(query_terms, 'video', scatter_dimension=1, tiled=True)]
    all_to_all x0 -> x2, blocking collectives: none -> 82.7 us  [the longest x1 44.9 us: local(): own = lax.all_to_all(send, PLANE, 0, 0, tiled=True)]
    psum x1 -> x0, blocking collectives: 60.2 us -> none  [local(): lax.psum((local_out * widen(factor), local_total * factor), 'video')]
    pmax x1 -> x0, blocking collectives: 55.8 us -> none  [local(): row_top = lax.pmax(local_peak, 'video')]
    dot_general x24 -> x0, matrix products: 28.9 us -> none  [the longest x4 8.49 us: local(): jnp.einsum('rhd,cd->rhc', grad_grp, value_grp, preferred_element_type=jnp...]
    unnamed x61 -> x6, local copies, waits for them, and re-layouts: 19.7 us -> 1.69 us
  transfers between devices with their start and end apart: 4 -> 2, of which waited for: 4 -> 1; matrix products, arithmetic and copies ran while one was open for 9% -> 2% of each run, Pallas kernels for 0% -> 0%
where the time goes in v1:
time: 102 us
  blocking collectives  82.7 us (81%)
  Pallas kernels  8.2 us (8%)
  local copies, waits for them, and re-layouts  3.71 us (4%)
  other arithmetic  3.34 us (3%)
  waiting for transfers between devices  2.5 us (2%)
    all_to_all x1, blocking collectives, local(): own = lax.all_to_all(send, PLANE, 0, 0, tiled=True)  44.9 us
    all_to_all x1, blocking collectives, local(): got = lax.all_to_all(part, PLANE, 0, 0, tiled=True)  37.8 us
    pallas_call x1, Pallas kernels, attend(): pl.pallas_call(kernel, out_shape=(jax.ShapeDtypeStruct((ROWS, HL * HD), j...  8.2 us
    ppermute x2, waiting for transfers between devices, swap(): return lax.ppermute(x, 'c', [(0, 1), (1, 0)])  2.5 us
  transfers between devices with their start and end apart: 2, of which 1 were waited for; matrix products, arithmetic and copies ran while one was open for 2% of the time, Pallas kernels for 0%

profile of v1, /device:TPU:8, one launch (start us, length us, event | category | flops | bytes accessed | tf_op | source)
XLA Modules:
  0.0 101.7 jit_solution(6529950102351748677)
XLA Ops:
  0.6 0.7 dynamic-slice_bitcast_fusion
  1.4 0.1 broadcast_in_dim.2
  1.5 44.9 %all_to_all.10.own_ref = f32[128,2,8,128]{3,2,1,0:T(8,128)S(1)} all-to-all(f32[128,2,8,128]{3,2,1,0:T(8,128)S(1)} %bitcast.21), channel_id=1, replica_groups=mesh['zl'=4,'y'=4,'c'=2,'x'=4,'zh'=2] {'zl','y','x','zh'}, dimensions={0} | all-to-all | bytes 2097152 | tf_op jit(solution)/shard_map/all_to_all | solution.py:131
  46.4 0.0 copy-start
  46.4 0.0 collective-permute-start
  46.4 0.0 copy-start.2
  46.4 0.7 copy-done.2
  47.1 0.6 fusion
  47.7 1.9 %pad_add_fusion.info = s32[4]{0:T(128)} fusion(s32[1]{0:T(128)} %bitcast.3, s32[1]{0:T(128)} %bitcast.2, s32[1]{0:T(128)} %bitcast.1, s32[1]{0:T(128)} %bitcast), kind=kLoop, calls=%fused_computation.6 | loop fusion | flops 12 | bytes 32 | tf_op jit(solution)/shard_map/stack | solution.py:133
  49.6 0.0 collective-permute-done.oth_ref
  49.6 0.0 copy-start.1
  49.6 0.0 copy-done
  49.6 1.0 %copy-done.1 = f32[128,2,8,128]{3,2,1,0:T(8,128)} copy-done((f32[128,2,8,128]{3,2,1,0:T(8,128)}, f32[128,2,8,128]{3,2,1,0:T(8,128)S(1)}, u32[]{:S(2)}) %copy-start.1) | copy-done | bytes 1048600
  50.6 8.2 %attend.1 = (bf16[128,512]{1,0:T(8,128)(2,1)}, bf16[128,512]{1,0:T(8,128)(2,1)}, f32[128,2,8,128]{3,2,1,0:T(8,128)}, f32[128,2,8,128]{3,2,1,0:T(8,128)}) custom-call(s32[4]{0:T(128)} %pad_add_fusion.info, bf16[128,4096]{1,0:T(8,128)(2,1)} %q_ref.1, bf16[128,4096]{1,0:T(8,128)(2,1)} %g_ref.1, f32[128,2,8,128]{3,2,1,0:T(8,128)} %copy-done, ...), custom_call_target="tpu_custom_call" | custom-call | tf_op jit(solution)/shard_map/attend/pallas_call | solution.py:94
  58.8 0.5 collective-permute-start.1
  59.3 2.5 %collective-permute-done.1 = f32[128,2,8,128]{3,2,1,0:T(8,128)S(1)} collective-permute-done((f32[128,2,8,128]{3,2,1,0:T(8,128)}, f32[128,2,8,128]{3,2,1,0:T(8,128)S(1)}, u32[]{:S(2)}, u32[]{:S(2)}) %collective-permute-start.1) | collective-permute-done | bytes 1048608 | tf_op jit(solution)/shard_map/ppermute | solution.py:119
  61.8 1.4 %add.20 = f32[128,2,8,128]{3,2,1,0:T(8,128)S(1)} add(f32[128,2,8,128]{3,2,1,0:T(8,128)} %get-tuple-element.10, f32[128,2,8,128]{3,2,1,0:T(8,128)S(1)} %collective-permute-done.1) | non-fusion elementwise | flops 262144 | bytes 3145728 | tf_op jit(solution)/shard_map/add | solution.py:135
  63.2 37.8 %all_to_all.11 = f32[128,2,8,128]{3,2,1,0:T(8,128)S(1)} all-to-all(f32[128,2,8,128]{3,2,1,0:T(8,128)S(1)} %add.20), channel_id=1, replica_groups=mesh['zl'=4,'y'=4,'c'=2,'x'=4,'zh'=2] {'zl','y','x','zh'}, dimensions={0} | all-to-all | bytes 2097152 | tf_op jit(solution)/shard_map/all_to_all | solution.py:136
  101.0 0.1 reduce_sum.9
  101.1 0.6 slice_bitcast_fusion
  (1 shorter events, 0.0 us)
Async XLA Ops:
  46.4 3.1 %copy-start = (f32[128,2,8,128]{3,2,1,0:T(8,128)}, f32[128,2,8,128]{3,2,1,0:T(8,128)S(1)}, u32[]{:S(2)}) copy-start(f32[128,2,8,128]{3,2,1,0:T(8,128)S(1)} %all_to_all.10.own_ref) | copy-start | bytes 3145732
  46.4 3.1 %collective-permute-start = (f32[128,2,8,128]{3,2,1,0:T(8,128)S(1)}, f32[128,2,8,128]{3,2,1,0:T(8,128)S(1)}, u32[]{:S(2)}, u32[]{:S(2)}) collective-permute-start(f32[128,2,8,128]{3,2,1,0:T(8,128)S(1)} %all_to_all.10.own_ref), channel_id=1, source_target_pairs={{0,8},{8,0},{1,9},{9,1},{2,10},{10,2},{3,11},{11,3},{4,12},{12,4},... | collective-permute-start | bytes 3145736 | tf_op jit(solution)/shard_map/ppermute | solution.py:119
  46.4 0.7 copy-start.2
  49.6 1.0 %copy-start.1 = (f32[128,2,8,128]{3,2,1,0:T(8,128)}, f32[128,2,8,128]{3,2,1,0:T(8,128)S(1)}, u32[]{:S(2)}) copy-start(f32[128,2,8,128]{3,2,1,0:T(8,128)S(1)} %collective-permute-done.oth_ref) | copy-start | bytes 3145732
  58.8 3.0 %collective-permute-start.1 = (f32[128,2,8,128]{3,2,1,0:T(8,128)}, f32[128,2,8,128]{3,2,1,0:T(8,128)S(1)}, u32[]{:S(2)}, u32[]{:S(2)}) collective-permute-start(f32[128,2,8,128]{3,2,1,0:T(8,128)} %get-tuple-element.11), channel_id=1, source_target_pairs={{0,8},{8,0},{1,9},{9,1},{2,10},{10,2},{3,11},{11,3},{4,12},{12,4},... | collective-permute-start | bytes 3145736 | tf_op jit(solution)/shard_map/ppermute | solution.py:119
